TPU v7x, 32 devices: a whole 2x2x4 slice. The times are simulated.
32 devices in a mesh: gy: 4 (over y, x), gx: 8 (over z, core).
Axes of the slice: x: 2, y: 2, z: 4, core: 2. Of those that a mesh axis runs over, the one named last changes fastest.
Arguments:
- cost_volume: int32 [64, 128, 256], P('gy', 'gx'), may hold values from 0 to 64
- left_image: float32 [64, 128], P('gy', 'gx'), may hold values from -6 to 6
- p_small: int32 [4], replicated, may hold values from 4 to 16
- p_large: int32 [4], replicated, may hold values from 32 to 128
Outputs:
- aggregated: float32 [64, 128, 256], P('gy', 'gx')
Inputs may be any that keep to these rules, and one draw needn't show every extreme that they name: `p_small`: every small penalty is below every large penalty.
All inputs are finite; a program needn't handle non-finite values.
Results may differ from a plain program's by a relative error of at most 0.00002.
Values sent between devices are 32-bit elements; how exact they have to be, the bound alone decides.
A program may use at most 64 MiB of HBM per device.

v0:
```python
import functools

import jax
import jax.numpy as jnp
from jax import lax
from jax.experimental import pallas as pl
from jax.experimental.pallas import tpu as pltpu
from jax.sharding import PartitionSpec as P

FAR = 1e30
GRADIENT_GAIN = 4.0
OUT_SCALE = 1.0 / 256.0
LANES = 128
SUBLANES = 8
BATCH = 4
UNROLL = 2
VMEM_BYTES = 20 << 20
MESH = pl.DeviceIdType.MESH


def tree_min(parts):
    parts = list(parts)
    while len(parts) > 1:
        pairs = [jnp.minimum(a, b) for a, b in zip(parts[::2], parts[1::2])]
        parts = pairs + ([parts[-1]] if len(parts) % 2 else [])
    return parts[0]


def all_sublanes_min(x):
    for by in (4, 2, 1):
        x = jnp.minimum(x, pltpu.roll(x, by, 0))
    return x


def kernel(
    rows,
    cols,
    cost_ref,
    image_hbm,
    small_hbm,
    large_hbm,
    out_ref,
    image_ref,
    small_ref,
    large_ref,
    staged,
    ordered,
    order,
    totals,
    costs,
    paths,
    lowests,
    large_lines,
    image_lines,
    outbox,
    inbox,
    edge_out,
    edge_in,
    send_sems,
    recv_sems,
    edge_send_sems,
    edge_recv_sems,
    local_sems,
):
    disparities = cost_ref.shape[1]
    nv = disparities // SUBLANES
    nx, ny = lax.axis_size("gx"), lax.axis_size("gy")
    ix, iy = lax.axis_index("gx"), lax.axis_index("gy")
    lines = (rows, rows, cols, cols)
    lengths = (cols, cols, rows, rows)
    backward = (False, True, False, True)
    targets = (
        {"gx": ix + 1},
        {"gx": ix - 1},
        {"gy": iy + 1},
        {"gy": iy - 1},
    )
    has_next = (ix < nx - 1, ix > 0, iy < ny - 1, iy > 0)
    has_prev = (ix > 0, ix < nx - 1, iy > 0, iy < ny - 1)

    halves = disparities // LANES

    def cost_copy(h):
        return pltpu.make_async_copy(
            cost_ref.at[:, pl.ds(h * LANES, LANES)], staged.at[h], local_sems.at[h]
        )

    small_copies = [
        pltpu.make_async_copy(source, target, local_sems.at[halves + at])
        for at, (source, target) in enumerate(
            ((image_hbm, image_ref), (small_hbm, small_ref), (large_hbm, large_ref))
        )
    ]
    for h in range(halves):
        cost_copy(h).start()
    for copy in small_copies:
        copy.start()

    barrier = pltpu.get_barrier_semaphore()
    for k in range(4):

        @pl.when(has_next[k])
        def _(k=k):
            pl.semaphore_signal(barrier, inc=1, device_id=targets[k], device_id_type=MESH)

    neighbours = sum(jnp.where(flag, 1, 0) for flag in has_next)

    shape = (disparities, disparities)
    source = lax.broadcasted_iota(jnp.int32, shape, 0)
    target = lax.broadcasted_iota(jnp.int32, shape, 1)
    wanted = target // SUBLANES + nv * (target % SUBLANES)
    order[...] = jnp.where(source == wanted, 1.0, 0.0).astype(jnp.bfloat16)

    for copy in small_copies:
        copy.wait()
    image = image_ref[...]
    image_lines[...] = jnp.zeros_like(image_lines)
    image_lines[0, :cols, :rows] = image.T
    image_lines[1, :rows, :cols] = image
    edge_out[...] = jnp.zeros_like(edge_out)
    for k in range(4):
        last = 0 if backward[k] else lengths[k] - 1
        edge_out[k, 0:1, :] = image_lines[k // 2, last : last + 1, :]

    def edge_copy(k):
        return pltpu.make_async_remote_copy(
            src_ref=edge_out.at[k],
            dst_ref=edge_in.at[k],
            send_sem=edge_send_sems.at[k],
            recv_sem=edge_recv_sems.at[k],
            device_id=targets[k],
            device_id_type=MESH,
        )

    def path_copy(k):
        return pltpu.make_async_remote_copy(
            src_ref=outbox.at[k],
            dst_ref=inbox.at[k],
            send_sem=send_sems.at[k],
            recv_sem=recv_sems.at[k],
            device_id=targets[k],
            device_id_type=MESH,
        )

    for h in range(halves):
        cost_copy(h).wait()

    block = jnp.concatenate([staged[h] for h in range(halves)], axis=1)
    block = block.astype(jnp.float32).astype(jnp.bfloat16)
    block = jnp.dot(block, order[...], preferred_element_type=jnp.float32)
    for h in range(halves):
        ordered[h] = block[:, h * LANES : (h + 1) * LANES]

    def turn_in(axis, line, at, count):
        per = LANES // SUBLANES
        for h in range(halves):
            block = ordered[h, at, :].T.reshape(per, SUBLANES, count)
            costs[axis, line, h * per : (h + 1) * per, :, :count] = block

    def turn_across(index, carry):
        for slot in range(BATCH):
            line = index * BATCH + slot
            turn_in(0, line, pl.ds(line, rows, stride=cols), rows)
        return carry

    def turn_down(index, carry):
        for slot in range(BATCH):
            line = index * BATCH + slot
            turn_in(1, line, pl.ds(pl.multiple_of(line * cols, cols), cols), cols)
        return carry

    lax.fori_loop(0, cols // BATCH, turn_across, 0)

    pl.semaphore_wait(barrier, neighbours)
    for k in range(4):

        @pl.when(has_next[k])
        def _(k=k):
            edge_copy(k).start()

    sub = lax.broadcasted_iota(jnp.int32, (SUBLANES, LANES), 0)
    lane = lax.broadcasted_iota(jnp.int32, (SUBLANES, LANES), 1)

    def turn_back(registers, count):
        per = LANES // SUBLANES
        return [
            jnp.concatenate(registers[h * per : (h + 1) * per], axis=0)[:, :count].T
            for h in range(halves)
        ]

    def task(k):
        axis = k // 2
        length, width = lengths[k], lines[k]
        group = LANES // width
        small = small_ref[k].astype(jnp.float32)
        large = large_ref[k].astype(jnp.float32)
        own = image_lines[axis, :length, :]

        @pl.when(has_prev[k])
        def _():
            edge_copy(k).wait_recv()

        @pl.when(jnp.logical_not(has_prev[k]))
        def _():
            edge_in[k] = jnp.zeros((SUBLANES, LANES), jnp.float32)
            inbox[k] = jnp.zeros(inbox.shape[1:], jnp.float32)

        edge = edge_in[k, 0:1, :]
        if backward[k]:
            before = jnp.concatenate([own[1:], edge], axis=0)
        else:
            before = jnp.concatenate([edge, own[:-1]], axis=0)
        large_lines[k] = small + (large - small) / (1.0 + GRADIENT_GAIN * jnp.abs(own - before))

        @pl.when(has_prev[k])
        def _():
            path_copy(k).wait_recv()

        state = []
        for v in range(nv):
            packed = inbox[k, v // group]
            shift = (v % group) * width
            state.append(pltpu.roll(packed, LANES - shift, 1) if shift else packed)

        def step(index, state):
            line = length - 1 - index if backward[k] else index
            capped = large_lines[k, pl.ds(line, SUBLANES, stride=0), :]
            lowest = all_sublanes_min(tree_min(state))
            capped = capped + lowest
            under = jnp.where(sub == 0, FAR, pltpu.roll(state[-1], 1, 0))
            over = jnp.where(sub == SUBLANES - 1, FAR, pltpu.roll(state[0], SUBLANES - 1, 0))
            fresh = []
            for v in range(nv):
                low = state[v - 1] if v else under
                high = state[v + 1] if v < nv - 1 else over
                near = jnp.minimum(state[v], jnp.minimum(low, high) + small)
                fresh.append(costs[axis, line, v] + jnp.minimum(near, capped))
            for v in range(nv):
                paths[k, line, v] = fresh[v]
            lowests[k, line] = lowest
            return tuple(fresh)

        def steps(index, state):
            for part in range(UNROLL):
                state = step(index * UNROLL + part, state)
            return state

        state = lax.fori_loop(0, length // UNROLL, steps, tuple(state))

        @pl.when(has_next[k])
        def _():
            above = lowests[k, 0 if backward[k] else length - 1]
            sent = [part - above for part in state]
            for slot in range(nv // group):
                packed = sent[slot * group]
                for g in range(1, group):
                    moved = pltpu.roll(sent[slot * group + g], g * width, 1)
                    packed = jnp.where(lane >= g * width, moved, packed)
                outbox[k, slot] = packed
            path_copy(k).start()

    def both_ways(k, line, count):
        above = lowests[k, line] + lowests[k + 1, line]
        return turn_back(
            [paths[k, line, v] + paths[k + 1, line, v] - above for v in range(nv)], count
        )

    def down_total(index, carry):
        for slot in range(BATCH):
            line = index * BATCH + slot
            at = pl.ds(pl.multiple_of(line * cols, cols), cols)
            for h, part in enumerate(both_ways(2, line, cols)):
                totals[1, h, at, :] = part
        return carry

    def across_total(index, carry):
        for slot in range(BATCH):
            line = index * BATCH + slot
            at = pl.ds(line, rows, stride=cols)
            for h, part in enumerate(both_ways(0, line, rows)):
                totals[0, h, at, :] = part
        return carry

    low_turn = jnp.minimum(ix, nx - 1 - ix)
    high_turn = jnp.maximum(ix, nx - 1 - ix)
    spare = jnp.where(low_turn >= 3, low_turn - 1, 2 * nx + 2 * ny)

    def one_turn(turn, carry):
        pl.when(turn == ix)(lambda: task(0))
        pl.when(turn == nx - 1 - ix)(lambda: task(1))
        taken = jnp.logical_or(turn == low_turn, turn == high_turn)
        taken = jnp.logical_or(taken, turn == spare)
        used = sum(jnp.where(at < turn, 1, 0) for at in (low_turn, high_turn, spare))
        free = jnp.where(taken, -1, turn - used)
        pl.when(free == 0)(lambda: lax.fori_loop(0, rows // BATCH, turn_down, None))
        pl.when(free == iy)(lambda: task(2))
        pl.when(free == ny - 1 - iy)(lambda: task(3))
        pl.when(free == ny)(lambda: lax.fori_loop(0, rows // BATCH, down_total, None))
        return carry

    lax.fori_loop(0, max(nx, ny + 4), one_turn, 0)
    lax.fori_loop(0, cols // BATCH, across_total, 0)
    rest = jnp.concatenate([totals[0, h] + totals[1, h] for h in range(halves)], axis=1)
    rest = rest * OUT_SCALE
    result = None
    for part in range(3):
        piece = rest.astype(jnp.bfloat16)
        moved = lax.dot_general(
            piece, order[...], (((1,), (1,)), ((), ())), preferred_element_type=jnp.float32
        )
        result = moved if part == 0 else result + moved
        if part < 2:
            rest = rest - piece.astype(jnp.float32)
    out_ref[...] = result

    for k in range(4):

        @pl.when(has_next[k])
        def _(k=k):
            edge_copy(k).wait_send()
            path_copy(k).wait_send()


def on_device(cost_volume, left_image, p_small, p_large):
    rows, cols, disparities = cost_volume.shape
    nv = disparities // SUBLANES
    longest = max(rows, cols)
    packed = nv * longest // LANES
    halves = disparities // LANES
    hbm = pl.BlockSpec(memory_space=pltpu.HBM)
    vmem = pl.BlockSpec(memory_space=pltpu.VMEM)
    total = pl.pallas_call(
        functools.partial(kernel, rows, cols),
        out_shape=jax.ShapeDtypeStruct((rows * cols, disparities), jnp.float32),
        in_specs=[hbm] * 4,
        out_specs=vmem,
        scratch_shapes=[
            pltpu.VMEM((rows, cols), jnp.float32),
            pltpu.SMEM((4,), jnp.int32),
            pltpu.SMEM((4,), jnp.int32),
            pltpu.VMEM((halves, rows * cols, LANES), jnp.int32),
            pltpu.VMEM((halves, rows * cols, LANES), jnp.float32),
            pltpu.VMEM((disparities, disparities), jnp.bfloat16),
            pltpu.VMEM((2, halves, rows * cols, LANES), jnp.float32),
            pltpu.VMEM((2, longest, nv, SUBLANES, LANES), jnp.float32),
            pltpu.VMEM((4, longest, nv, SUBLANES, LANES), jnp.float32),
            pltpu.VMEM((4, longest, SUBLANES, LANES), jnp.float32),
            pltpu.VMEM((4, longest, LANES), jnp.float32),
            pltpu.VMEM((2, longest, LANES), jnp.float32),
            pltpu.VMEM((4, packed, SUBLANES, LANES), jnp.float32),
            pltpu.VMEM((4, packed, SUBLANES, LANES), jnp.float32),
            pltpu.VMEM((4, SUBLANES, LANES), jnp.float32),
            pltpu.VMEM((4, SUBLANES, LANES), jnp.float32),
            pltpu.SemaphoreType.DMA((4,)),
            pltpu.SemaphoreType.DMA((4,)),
            pltpu.SemaphoreType.DMA((4,)),
            pltpu.SemaphoreType.DMA((4,)),
            pltpu.SemaphoreType.DMA((halves + 3,)),
        ],
        compiler_params=pltpu.CompilerParams(
            collective_id=0, has_side_effects=True, vmem_limit_bytes=VMEM_BYTES
        ),
    )(
        *(
            pltpu.with_memory_space_constraint(array, pltpu.HBM)
            for array in (
                cost_volume.reshape(rows * cols, disparities),
                left_image,
                p_small,
                p_large,
            )
        )
    )
    return total.reshape(rows, cols, disparities)


def solution(mesh):
    in_specs = (P("gy", "gx", None), P("gy", "gx"), P(), P())
    out_specs = P("gy", "gx", None)
    return jax.shard_map(
        on_device, mesh=mesh, in_specs=in_specs, out_specs=out_specs, check_vma=False
    )
```

profile of v0, /device:TPU:0, one launch (start us, length us, event | category | flops | bytes accessed | tf_op | source)
XLA Modules:
  0.0 24.9 jit_solution(11988005964498058366)
XLA Ops:
  0.0 24.2 %shard_map.46 = f32[256,256]{1,0:T(8,128)S(1)} custom-call(s32[256,256]{1,0:T(8,128)} %bitcast.3, f32[16,16]{1,0:T(8,128)} %image_hbm.1, s32[4]{0:T(128)} %small_hbm.1, s32[4]{0:T(128)} %large_hbm.1), custom_call_target="tpu_custom_call" | custom-call | tf_op jit(solution)/shard_map/pallas_call | solution.py:332
  24.2 0.7 %copy.6 = f32[16,16,256]{2,1,0:T(8,128)} copy(f32[16,16,256]{2,1,0:T(8,128)S(1)} %bitcast.2) | data formatting | bytes 524288
where the time goes:
time: 25 us; the launch traced here: 24.9 us
  Pallas kernels  24.2 us (97%)
  local copies, waits for them, and re-layouts  0.71 us (3%)
    pallas_call x1, Pallas kernels, on_device(): pl.pallas_call(functools.partial(kernel, rows, cols), out_shape=jax.Shape...  24.2 us
    unnamed x1, local copies, waits for them, and re-layouts  0.71 us

commit v1 on v0

v1 whole, which is shorter than its diff:
```python
import functools

import jax
import jax.numpy as jnp
from jax import lax
from jax.experimental import pallas as pl
from jax.experimental.pallas import tpu as pltpu
from jax.sharding import PartitionSpec as P

FAR = 1e30
GRADIENT_GAIN = 4.0
OUT_SCALE = 1.0 / 256.0
LANES = 128
SUBLANES = 8
BATCH = 4
UNROLL = 2
CORES = 2
VMEM_BYTES = 40 << 20
MESH = pl.DeviceIdType.MESH


def tree_min(parts):
    parts = list(parts)
    while len(parts) > 1:
        pairs = [jnp.minimum(a, b) for a, b in zip(parts[::2], parts[1::2])]
        parts = pairs + ([parts[-1]] if len(parts) % 2 else [])
    return parts[0]


def all_sublanes_min(x):
    for by in (4, 2, 1):
        x = jnp.minimum(x, pltpu.roll(x, by, 0))
    return x


def kernel(
    rows,
    cols,
    cost_hbm,
    image_hbm,
    small_hbm,
    large_hbm,
    out_ref,
    small_ref,
    large_ref,
    own_image,
    mate_image,
    own_raw,
    mate_raw,
    far_raw,
    ordered,
    ordered_other,
    order,
    totals,
    across_costs,
    down_costs,
    paths,
    lowests,
    large_lines,
    image_lines,
    outbox,
    inbox,
    edge_out,
    edge_in,
    send_sems,
    recv_sems,
    local_sems,
):
    disparities = cost_hbm.shape[1]
    nv = disparities // SUBLANES
    halves = disparities // LANES
    nx, ny = lax.axis_size("gx"), lax.axis_size("gy")
    ix, iy = lax.axis_index("gx"), lax.axis_index("gy")
    nz = nx // CORES
    iz, core = ix // CORES, ix % CORES
    mate = {"gx": iz * CORES + 1 - core}
    own_base = core * cols
    costs = (across_costs, down_costs)
    lengths = (cols, cols, rows, rows)
    lines = (rows, rows, cols, cols)
    backward = (False, True, False, True)

    place = (iz, nz - 1 - iz, iy, ny - 1 - iy)
    places = (nz, nz, ny, ny)
    hands_on = (core == 1, core == 0, True, True)
    is_last = [place[k] == places[k] - 1 for k in range(4)]
    skips = (False, False, places[2] > 1, places[3] > 1)

    def next_across(k, to_core):
        step = -1 if backward[k] else 1
        return {"gx": (iz + step) * CORES + to_core}

    def next_down(k, by):
        return {"gy": iy - by if backward[k] else iy + by}

    def prev_across(k):
        return {"gx": (iz + 1) * CORES if backward[k] else (iz - 1) * CORES + 1}

    def both(*flags):
        result = True
        for flag in flags:
            result = flag if result is True else jnp.logical_and(result, flag)
        return result

    def remote(source, target, send, recv, device):
        return pltpu.make_async_remote_copy(
            src_ref=source,
            dst_ref=target,
            send_sem=send_sems.at[send],
            recv_sem=recv_sems.at[recv],
            device_id=device,
            device_id_type=MESH,
        )

    mate_copies = [
        (None, remote(own_image, mate_image, 0, 0, mate)),
        (None, remote(own_raw, mate_raw, 1, 1, mate)),
    ]
    edge_copies, path_copies = [], []
    edge_recv, path_recv, far_recv = [], [], []
    far_raw_copies, far_large_copies = {}, {}
    for k in range(4):
        if k < 2:
            has_next = jnp.logical_and(place[k] < places[k] - 1, hands_on[k])
            e = [
                (has_next, remote(edge_out.at[k], edge_in.at[k], 2 + 2 * k + to, 2 + k, next_across(k, to)))
                for to in range(CORES)
            ]
            p = [
                (has_next, remote(outbox.at[k], inbox.at[k], 10 + 2 * k + to, 6 + k, next_across(k, to)))
                for to in range(CORES)
            ]
        else:
            has_next = place[k] < places[k] - 1
            e = [(has_next, remote(edge_out.at[k], edge_in.at[k], 2 + 2 * k, 2 + k, next_down(k, 1)))]
            p = [
                (
                    place[k] < places[k] - 2,
                    remote(outbox.at[k], inbox.at[k], 10 + 2 * k, 6 + k, next_down(k, 1)),
                ),
                (
                    place[k] == places[k] - 3,
                    remote(outbox.at[k], inbox.at[k], 11 + 2 * k, 6 + k, next_down(k, 2)),
                ),
            ]
            before_last = place[k] == places[k] - 2
            far_raw_copies[k] = (before_last, remote(own_raw, far_raw, 18 + k - 2, 10, next_down(k, 1)))
            far_large_copies[k] = (
                before_last,
                remote(
                    large_lines.at[k, pl.ds(rows, rows)],
                    large_lines.at[k, pl.ds(0, rows)],
                    20 + k - 2,
                    11,
                    next_down(k, 1),
                ),
            )
        edge_copies.append(e)
        path_copies.append(p)

    def start(copies):
        for flag, copy in copies:
            if flag is None:
                copy.start()
            else:
                pl.when(flag)(copy.start)

    def drain(copies):
        for flag, copy in copies:
            if flag is None:
                copy.wait_send()
            else:
                pl.when(flag)(copy.wait_send)

    locals_ = [
        pltpu.make_async_copy(source, target, local_sems.at[at])
        for at, (source, target) in enumerate(
            (
                (image_hbm, own_image),
                (small_hbm, small_ref),
                (large_hbm, large_ref),
                (cost_hbm, own_raw),
            )
        )
    ]
    for copy in locals_:
        copy.start()

    barrier = pltpu.get_barrier_semaphore()

    def greet(device):
        pl.semaphore_signal(barrier, inc=1, device_id=device, device_id_type=MESH)

    greet(mate)
    awaited = jnp.int32(1)
    for k in range(2):
        pl.when(place[k] > 0)(functools.partial(greet, prev_across(k)))
        sends = jnp.logical_and(place[k] < places[k] - 1, hands_on[k])
        awaited += jnp.where(sends, CORES, 0)
    for k in range(2, 4):
        pl.when(place[k] > 0)(functools.partial(greet, next_down(k, -1)))
        pl.when(jnp.logical_and(is_last[k], place[k] > 1))(
            functools.partial(greet, next_down(k, -2))
        )
        awaited += jnp.where(place[k] < places[k] - 1, 1, 0)
        awaited += jnp.where(place[k] == places[k] - 3, 1, 0)

    shape = (disparities, disparities)
    source = lax.broadcasted_iota(jnp.int32, shape, 0)
    target = lax.broadcasted_iota(jnp.int32, shape, 1)
    wanted = target // SUBLANES + nv * (target % SUBLANES)
    order[...] = jnp.where(source == wanted, 1.0, 0.0).astype(jnp.bfloat16)

    for copy in locals_[:3]:
        copy.wait()
    image = own_image[...]
    image_lines[...] = jnp.zeros_like(image_lines)
    image_lines[1, 0:rows, :cols] = image
    image_lines[0, pl.ds(pl.multiple_of(own_base, SUBLANES), cols), :rows] = image.T
    edge_out[...] = jnp.zeros_like(edge_out)
    edge_out[0, 0:1, :rows] = image.T[cols - 1 : cols, :]
    edge_out[1, 0:1, :rows] = image.T[0:1, :]
    edge_out[2, 0:1, :cols] = image[rows - 1 : rows, :]
    edge_out[3, 0:1, :cols] = image[0:1, :]
    locals_[3].wait()

    def reorder(raw, into):
        block = raw[...].astype(jnp.float32).astype(jnp.bfloat16)
        block = jnp.dot(block, order[...], preferred_element_type=jnp.float32)
        for h in range(halves):
            into[h] = block[:, h * LANES : (h + 1) * LANES]

    def turn_in(origin, into, line, at, count):
        per = LANES // SUBLANES
        for h in range(halves):
            block = origin[h, at, :].T.reshape(per, SUBLANES, count)
            into[line, h * per : (h + 1) * per, :, :count] = block

    def turn_across(origin, base):
        def some(index, carry):
            for slot in range(BATCH):
                line = index * BATCH + slot
                turn_in(origin, across_costs, base + line, pl.ds(line, rows, stride=cols), rows)
            return carry

        lax.fori_loop(0, cols // BATCH, some, 0)

    def turn_down(origin, base):
        def some(index, carry):
            for slot in range(BATCH):
                line = index * BATCH + slot
                at = pl.ds(pl.multiple_of(line * cols, cols), cols)
                turn_in(origin, down_costs, base + line, at, cols)
            return carry

        lax.fori_loop(0, rows // BATCH, some, 0)

    pl.semaphore_wait(barrier, awaited)
    start(mate_copies)
    for k in range(4):
        start(edge_copies[k])
    for k in range(2, 4):
        start([far_raw_copies[k]])

    reorder(own_raw, ordered)
    turn_down(ordered, rows)
    turn_across(ordered, own_base)

    sub = lax.broadcasted_iota(jnp.int32, (SUBLANES, LANES), 0)
    lane = lax.broadcasted_iota(jnp.int32, (SUBLANES, LANES), 1)

    def turn_back(registers, count):
        per = LANES // SUBLANES
        return [
            jnp.concatenate(registers[h * per : (h + 1) * per], axis=0)[:, :count].T
            for h in range(halves)
        ]

    def task(k):
        axis = k // 2
        length, width = lengths[k], lines[k]
        group = LANES // width
        small = small_ref[k].astype(jnp.float32)
        large = large_ref[k].astype(jnp.float32)
        step_costs = costs[axis]
        first = place[k] == 0

        @pl.when(jnp.logical_not(first))
        def _():
            edge_copies[k][0][1].wait_recv()

        @pl.when(first)
        def _():
            edge_in[k] = jnp.zeros((SUBLANES, LANES), jnp.float32)

        edge = edge_in[k, 0:1, :]
        if axis == 0:
            own = image_lines[0, : 2 * length, :]
        else:
            own = image_lines[1, :length, :]
        if backward[k]:
            before = jnp.concatenate([own[1:], edge], axis=0)
        else:
            before = jnp.concatenate([edge, own[:-1]], axis=0)
        found = small + (large - small) / (1.0 + GRADIENT_GAIN * jnp.abs(own - before))
        if axis == 0:
            large_lines[k, : 2 * length] = found
        else:
            large_lines[k, length : 2 * length] = found
            start([far_large_copies[k]])

            @pl.when(jnp.logical_and(is_last[k], jnp.logical_not(first)))
            def _():
                far_raw_copies[k][1].wait_recv()
                reorder(far_raw, ordered_other)
                turn_down(ordered_other, 0)
                far_large_copies[k][1].wait_recv()

        if axis == 0:
            receives = jnp.logical_not(first)
        else:
            receives = jnp.logical_or(
                jnp.logical_and(place[k] > 0, jnp.logical_not(is_last[k])),
                jnp.logical_and(is_last[k], place[k] > 1),
            )

        @pl.when(receives)
        def _():
            path_copies[k][0][1].wait_recv()

        @pl.when(jnp.logical_not(receives))
        def _():
            inbox[k] = jnp.zeros(inbox.shape[1:], jnp.float32)

        state = []
        for v in range(nv):
            packed = inbox[k, v // group]
            shift = (v % group) * width
            state.append(pltpu.roll(packed, LANES - shift, 1) if shift else packed)

        def step(line, state):
            capped = large_lines[k, pl.ds(line, SUBLANES, stride=0), :]
            under = jnp.where(sub == 0, FAR, pltpu.roll(state[-1], 1, 0))
            over = jnp.where(sub == SUBLANES - 1, FAR, pltpu.roll(state[0], SUBLANES - 1, 0))
            beside = []
            for v in range(nv):
                low = state[v - 1] if v else under
                high = state[v + 1] if v < nv - 1 else over
                beside.append(jnp.minimum(low, high))
            if nv % 4 == 0:
                lowest = tree_min([beside[v] for v in range(nv) if v % 4 in (1, 2)])
            else:
                lowest = tree_min(state)
            lowest = all_sublanes_min(lowest)
            capped = capped + lowest
            fresh = []
            for v in range(nv):
                near = jnp.minimum(state[v], beside[v] + small)
                fresh.append(step_costs[line, v] + jnp.minimum(near, capped))
            return tuple(fresh), lowest

        def early(index, state):
            for part in range(UNROLL):
                at = index * UNROLL + part
                if axis == 0:
                    line = 2 * length - 1 - at if backward[k] else at
                else:
                    line = length - 1 - at if backward[k] else at
                state, _ = step(line, state)
            return state

        def late(index, state):
            for part in range(UNROLL):
                at = index * UNROLL + part
                at = length - 1 - at if backward[k] else at
                state, lowest = step((own_base if axis == 0 else length) + at, state)
                for v in range(nv):
                    paths[k, at, v] = state[v]
                lowests[k, at] = lowest
            return state

        if axis == 0:
            ahead = jnp.where(hands_on[k], length // UNROLL, 0)
        else:
            ahead = jnp.where(jnp.logical_and(is_last[k], place[k] > 0), length // UNROLL, 0)
        state = lax.fori_loop(0, ahead, early, tuple(state))
        state = lax.fori_loop(0, length // UNROLL, late, tuple(state))

        if axis == 0:
            sends = path_copies[k][0][0]
        else:
            sends = jnp.logical_or(path_copies[k][0][0], path_copies[k][1][0])

        @pl.when(sends)
        def _():
            above = lowests[k, 0 if backward[k] else length - 1]
            sent = [part - above for part in state]
            for slot in range(nv // group):
                packed = sent[slot * group]
                for g in range(1, group):
                    moved = pltpu.roll(sent[slot * group + g], g * width, 1)
                    packed = jnp.where(lane >= g * width, moved, packed)
                outbox[k, slot] = packed

        start(path_copies[k])

    def both_ways(k, line, count):
        above = lowests[k, line] + lowests[k + 1, line]
        return turn_back(
            [paths[k, line, v] + paths[k + 1, line, v] - above for v in range(nv)], count
        )

    def down_total():
        def some(index, carry):
            for slot in range(BATCH):
                line = index * BATCH + slot
                at = pl.ds(pl.multiple_of(line * cols, cols), cols)
                for h, part in enumerate(both_ways(2, line, cols)):
                    totals[1, h, at, :] = part
            return carry

        lax.fori_loop(0, rows // BATCH, some, 0)

    def across_total():
        def some(index, carry):
            for slot in range(BATCH):
                line = index * BATCH + slot
                at = pl.ds(line, rows, stride=cols)
                for h, part in enumerate(both_ways(0, line, rows)):
                    totals[0, h, at, :] = part
            return carry

        lax.fori_loop(0, cols // BATCH, some, 0)

    turns = max(nz, ny)
    down_done = jnp.maximum(place[2], place[3])

    def one_turn(turn, carry):
        pl.when(turn == place[2])(lambda: task(2))
        pl.when(turn == place[3])(lambda: task(3))

        @pl.when(turn == 0)
        def _():
            for _, copy in mate_copies:
                copy.wait_recv()
            at = pl.ds(pl.multiple_of(cols - own_base, SUBLANES), cols)
            image_lines[0, at, :rows] = mate_image[...].T
            reorder(mate_raw, ordered_other)
            turn_across(ordered_other, cols - own_base)

        at_end = jnp.logical_and(turn == down_done, turn == turns - 1)
        pl.when(at_end)(down_total)
        pl.when(turn == place[0])(lambda: task(0))
        pl.when(turn == place[1])(lambda: task(1))
        before_end = jnp.logical_and(turn == down_done, turn < turns - 1)
        pl.when(before_end)(down_total)
        return carry

    lax.fori_loop(0, turns, one_turn, 0)
    across_total()
    rest = jnp.concatenate([totals[0, h] + totals[1, h] for h in range(halves)], axis=1)
    rest = rest * OUT_SCALE
    result = None
    for part in range(3):
        piece = rest.astype(jnp.bfloat16)
        moved = lax.dot_general(
            piece, order[...], (((1,), (1,)), ((), ())), preferred_element_type=jnp.float32
        )
        result = moved if part == 0 else result + moved
        if part < 2:
            rest = rest - piece.astype(jnp.float32)
    out_ref[...] = result

    drain(mate_copies)
    for k in range(4):
        drain(edge_copies[k])
        drain(path_copies[k])
    for k in range(2, 4):
        drain([far_raw_copies[k], far_large_copies[k]])


def on_device(cost_volume, left_image, p_small, p_large):
    rows, cols, disparities = cost_volume.shape
    nv = disparities // SUBLANES
    longest = max(rows, cols)
    packed = nv * longest // LANES
    halves = disparities // LANES
    block = (rows * cols, disparities)
    hbm = pl.BlockSpec(memory_space=pltpu.HBM)
    vmem = pl.BlockSpec(memory_space=pltpu.VMEM)
    total = pl.pallas_call(
        functools.partial(kernel, rows, cols),
        out_shape=jax.ShapeDtypeStruct((rows * cols, disparities), jnp.float32),
        in_specs=[hbm] * 4,
        out_specs=vmem,
        scratch_shapes=[
            pltpu.SMEM((4,), jnp.int32),
            pltpu.SMEM((4,), jnp.int32),
            pltpu.VMEM((rows, cols), jnp.float32),
            pltpu.VMEM((rows, cols), jnp.float32),
            pltpu.VMEM(block, jnp.int32),
            pltpu.VMEM(block, jnp.int32),
            pltpu.VMEM(block, jnp.int32),
            pltpu.VMEM((halves, rows * cols, LANES), jnp.float32),
            pltpu.VMEM((halves, rows * cols, LANES), jnp.float32),
            pltpu.VMEM((disparities, disparities), jnp.bfloat16),
            pltpu.VMEM((2, halves, rows * cols, LANES), jnp.float32),
            pltpu.VMEM((2 * cols, nv, SUBLANES, LANES), jnp.float32),
            pltpu.VMEM((2 * rows, nv, SUBLANES, LANES), jnp.float32),
            pltpu.VMEM((4, longest, nv, SUBLANES, LANES), jnp.float32),
            pltpu.VMEM((4, longest, SUBLANES, LANES), jnp.float32),
            pltpu.VMEM((4, 2 * longest, LANES), jnp.float32),
            pltpu.VMEM((2, 2 * longest, LANES), jnp.float32),
            pltpu.VMEM((4, packed, SUBLANES, LANES), jnp.float32),
            pltpu.VMEM((4, packed, SUBLANES, LANES), jnp.float32),
            pltpu.VMEM((4, SUBLANES, LANES), jnp.float32),
            pltpu.VMEM((4, SUBLANES, LANES), jnp.float32),
            pltpu.SemaphoreType.DMA((22,)),
            pltpu.SemaphoreType.DMA((12,)),
            pltpu.SemaphoreType.DMA((4,)),
        ],
        compiler_params=pltpu.CompilerParams(
            collective_id=0, has_side_effects=True, vmem_limit_bytes=VMEM_BYTES
        ),
    )(
        *(
            pltpu.with_memory_space_constraint(array, pltpu.HBM)
            for array in (
                cost_volume.reshape(rows * cols, disparities),
                left_image,
                p_small,
                p_large,
            )
        )
    )
    return total.reshape(rows, cols, disparities)


def solution(mesh):
    in_specs = (P("gy", "gx", None), P("gy", "gx"), P(), P())
    out_specs = P("gy", "gx", None)
    return jax.shard_map(
        on_device, mesh=mesh, in_specs=in_specs, out_specs=out_specs, check_vma=False
    )
```

time: 25 us -> 23.8 us (0.952)
  Pallas kernels: 24.2 us -> 22.9 us
    pallas_call x1, Pallas kernels: 24.2 us -> 22.9 us  [on_device(): pl.pallas_call(functools.partial(kernel, rows, cols), out_shape=jax.Shape...]
where the time goes in v1:
time: 23.8 us; the launch traced here: 23.6 us
  Pallas kernels  22.9 us (96%)
  local copies, waits for them, and re-layouts  0.71 us (3%)
    pallas_call x1, Pallas kernels, on_device(): pl.pallas_call(functools.partial(kernel, rows, cols), out_shape=jax.Shape...  22.9 us
    unnamed x1, local copies, waits for them, and re-layouts  0.71 us

profile of v1, /device:TPU:0, one launch (start us, length us, event | category | flops | bytes accessed | tf_op | source)
XLA Modules:
  0.0 23.6 jit_solution(4071627429073928522)
XLA Ops:
  0.0 22.9 %shard_map.46 = f32[256,256]{1,0:T(8,128)S(1)} custom-call(s32[256,256]{1,0:T(8,128)} %bitcast.3, f32[16,16]{1,0:T(8,128)} %image_hbm.1, s32[4]{0:T(128)} %small_hbm.1, s32[4]{0:T(128)} %large_hbm.1), custom_call_target="tpu_custom_call" | custom-call | tf_op jit(solution)/shard_map/pallas_call | solution.py:491
  22.9 0.7 %copy.6 = f32[16,16,256]{2,1,0:T(8,128)} copy(f32[16,16,256]{2,1,0:T(8,128)S(1)} %bitcast.2) | data formatting | bytes 524288

commit v2 on v1

--- a/solution.py
+++ b/solution.py
@@ -48,8 +48,6 @@
     own_raw,
     mate_raw,
     far_raw,
-    ordered,
-    ordered_other,
     order,
     totals,
     across_costs,
@@ -179,7 +177,10 @@
                 (image_hbm, own_image),
                 (small_hbm, small_ref),
                 (large_hbm, large_ref),
-                (cost_hbm, own_raw),
+                *(
+                    (cost_hbm.at[:, pl.ds(h * LANES, LANES)], own_raw.at[h])
+                    for h in range(halves)
+                ),
             )
         )
     ]
@@ -206,8 +207,8 @@
         awaited += jnp.where(place[k] == places[k] - 3, 1, 0)
 
     shape = (disparities, disparities)
-    source = lax.broadcasted_iota(jnp.int32, shape, 0)
-    target = lax.broadcasted_iota(jnp.int32, shape, 1)
+    source = lax.broadcasted_iota(jnp.int32, shape, 1)
+    target = lax.broadcasted_iota(jnp.int32, shape, 0)
     wanted = target // SUBLANES + nv * (target % SUBLANES)
     order[...] = jnp.where(source == wanted, 1.0, 0.0).astype(jnp.bfloat16)
 
@@ -222,19 +223,16 @@
     edge_out[1, 0:1, :rows] = image.T[0:1, :]
     edge_out[2, 0:1, :cols] = image[rows - 1 : rows, :]
     edge_out[3, 0:1, :cols] = image[0:1, :]
-    locals_[3].wait()
-
-    def reorder(raw, into):
-        block = raw[...].astype(jnp.float32).astype(jnp.bfloat16)
-        block = jnp.dot(block, order[...], preferred_element_type=jnp.float32)
-        for h in range(halves):
-            into[h] = block[:, h * LANES : (h + 1) * LANES]
+    for copy in locals_[3:]:
+        copy.wait()
 
     def turn_in(origin, into, line, at, count):
-        per = LANES // SUBLANES
-        for h in range(halves):
-            block = origin[h, at, :].T.reshape(per, SUBLANES, count)
-            into[line, h * per : (h + 1) * per, :, :count] = block
+        block = jnp.concatenate([origin[h, at, :] for h in range(halves)], axis=1)
+        block = block.astype(jnp.float32).astype(jnp.bfloat16)
+        block = lax.dot_general(
+            order[...], block, (((1,), (1,)), ((), ())), preferred_element_type=jnp.float32
+        )
+        into[line, :, :, :count] = block.reshape(nv, SUBLANES, count)
 
     def turn_across(origin, base):
         def some(index, carry):
@@ -255,6 +253,18 @@
 
         lax.fori_loop(0, rows // BATCH, some, 0)
 
+    def take_mate():
+        for _, copy in mate_copies:
+            copy.wait_recv()
+        at = pl.ds(pl.multiple_of(cols - own_base, SUBLANES), cols)
+        image_lines[0, at, :rows] = mate_image[...].T
+        turn_across(mate_raw, cols - own_base)
+
+    @pl.when(iz < nz - 1)
+    def _():
+        turn_down(own_raw, rows)
+        turn_across(own_raw, own_base)
+
     pl.semaphore_wait(barrier, awaited)
     start(mate_copies)
     for k in range(4):
@@ -262,9 +272,10 @@
     for k in range(2, 4):
         start([far_raw_copies[k]])
 
-    reorder(own_raw, ordered)
-    turn_down(ordered, rows)
-    turn_across(ordered, own_base)
+    @pl.when(iz == nz - 1)
+    def _():
+        turn_across(own_raw, own_base)
+        take_mate()
 
     sub = lax.broadcasted_iota(jnp.int32, (SUBLANES, LANES), 0)
     lane = lax.broadcasted_iota(jnp.int32, (SUBLANES, LANES), 1)
@@ -312,8 +323,7 @@
             @pl.when(jnp.logical_and(is_last[k], jnp.logical_not(first)))
             def _():
                 far_raw_copies[k][1].wait_recv()
-                reorder(far_raw, ordered_other)
-                turn_down(ordered_other, 0)
+                turn_down(far_raw, 0)
                 far_large_copies[k][1].wait_recv()
 
         if axis == 0:
@@ -434,29 +444,19 @@
 
     turns = max(nz, ny)
     down_done = jnp.maximum(place[2], place[3])
+    turn_left = jnp.where(iz == 0, nz, place[1])
 
     def one_turn(turn, carry):
+        pl.when(turn == turn_left)(lambda: task(1))
+        pl.when(jnp.logical_and(turn == 0, iz == nz - 1))(lambda: turn_down(own_raw, rows))
         pl.when(turn == place[2])(lambda: task(2))
         pl.when(turn == place[3])(lambda: task(3))
-
-        @pl.when(turn == 0)
-        def _():
-            for _, copy in mate_copies:
-                copy.wait_recv()
-            at = pl.ds(pl.multiple_of(cols - own_base, SUBLANES), cols)
-            image_lines[0, at, :rows] = mate_image[...].T
-            reorder(mate_raw, ordered_other)
-            turn_across(ordered_other, cols - own_base)
-
-        at_end = jnp.logical_and(turn == down_done, turn == turns - 1)
-        pl.when(at_end)(down_total)
+        pl.when(jnp.logical_and(turn == 0, iz < nz - 1))(take_mate)
+        pl.when(turn == down_done)(down_total)
         pl.when(turn == place[0])(lambda: task(0))
-        pl.when(turn == place[1])(lambda: task(1))
-        before_end = jnp.logical_and(turn == down_done, turn < turns - 1)
-        pl.when(before_end)(down_total)
         return carry
 
-    lax.fori_loop(0, turns, one_turn, 0)
+    lax.fori_loop(0, turns + 1, one_turn, 0)
     across_total()
     rest = jnp.concatenate([totals[0, h] + totals[1, h] for h in range(halves)], axis=1)
     rest = rest * OUT_SCALE
@@ -464,7 +464,7 @@
     for part in range(3):
         piece = rest.astype(jnp.bfloat16)
         moved = lax.dot_general(
-            piece, order[...], (((1,), (1,)), ((), ())), preferred_element_type=jnp.float32
+            piece, order[...], (((1,), (0,)), ((), ())), preferred_element_type=jnp.float32
         )
         result = moved if part == 0 else result + moved
         if part < 2:
@@ -485,7 +485,7 @@
     longest = max(rows, cols)
     packed = nv * longest // LANES
     halves = disparities // LANES
-    block = (rows * cols, disparities)
+    block = (halves, rows * cols, LANES)
     hbm = pl.BlockSpec(memory_space=pltpu.HBM)
     vmem = pl.BlockSpec(memory_space=pltpu.VMEM)
     total = pl.pallas_call(
@@ -501,8 +501,6 @@
             pltpu.VMEM(block, jnp.int32),
             pltpu.VMEM(block, jnp.int32),
             pltpu.VMEM(block, jnp.int32),
-            pltpu.VMEM((halves, rows * cols, LANES), jnp.float32),
-            pltpu.VMEM((halves, rows * cols, LANES), jnp.float32),
             pltpu.VMEM((disparities, disparities), jnp.bfloat16),
             pltpu.VMEM((2, halves, rows * cols, LANES), jnp.float32),
             pltpu.VMEM((2 * cols, nv, SUBLANES, LANES), jnp.float32),
@@ -517,7 +515,7 @@
             pltpu.VMEM((4, SUBLANES, LANES), jnp.float32),
             pltpu.SemaphoreType.DMA((22,)),
             pltpu.SemaphoreType.DMA((12,)),
-            pltpu.SemaphoreType.DMA((4,)),
+            pltpu.SemaphoreType.DMA((3 + halves,)),
         ],
         compiler_params=pltpu.CompilerParams(
             collective_id=0, has_side_effects=True, vmem_limit_bytes=VMEM_BYTES

time: 23.8 us -> 22.5 us (0.945)
  Pallas kernels: 22.9 us -> 21.5 us
    pallas_call x1, Pallas kernels: 22.9 us -> 21.5 us  [on_device(): pl.pallas_call(functools.partial(kernel, rows, cols), out_shape=jax.Shape...]
where the time goes in v2:
time: 22.5 us; the launch traced here: 22.3 us
  Pallas kernels  21.5 us (96%)
  local copies, waits for them, and re-layouts  0.71 us (3%)
    pallas_call x1, Pallas kernels, on_device(): pl.pallas_call(functools.partial(kernel, rows, cols), out_shape=jax.Shape...  21.5 us
    unnamed x1, local copies, waits for them, and re-layouts  0.71 us

profile of v2, /device:TPU:0, one launch (start us, length us, event | category | flops | bytes accessed | tf_op | source)
XLA Modules:
  0.0 22.3 jit_solution(2184572346807051530)
XLA Ops:
  0.0 21.5 %shard_map.46 = f32[256,256]{1,0:T(8,128)S(1)} custom-call(s32[256,256]{1,0:T(8,128)} %bitcast.3, f32[16,16]{1,0:T(8,128)} %image_hbm.1, s32[4]{0:T(128)} %small_hbm.1, s32[4]{0:T(128)} %large_hbm.1), custom_call_target="tpu_custom_call" | custom-call | tf_op jit(solution)/shard_map/pallas_call | solution.py:491
  21.6 0.7 %copy.6 = f32[16,16,256]{2,1,0:T(8,128)} copy(f32[16,16,256]{2,1,0:T(8,128)S(1)} %bitcast.2) | data formatting | bytes 524288

commit v3 on v2

v3 whole, which is shorter than its diff:
```python
import functools

import jax
import jax.numpy as jnp
from jax import lax
from jax.experimental import pallas as pl
from jax.experimental.pallas import tpu as pltpu
from jax.sharding import PartitionSpec as P

FAR = 1e30
GRADIENT_GAIN = 4.0
OUT_SCALE = 1.0 / 256.0
LANES = 128
SUBLANES = 8
UNROLL = 2
CORES = 2
SENDS = 30
VMEM_BYTES = 40 << 20
SKIPS = (False, True, True, True)
MESH = pl.DeviceIdType.MESH


def tree_min(parts):
    parts = list(parts)
    while len(parts) > 1:
        pairs = [jnp.minimum(a, b) for a, b in zip(parts[::2], parts[1::2])]
        parts = pairs + ([parts[-1]] if len(parts) % 2 else [])
    return parts[0]


def all_sublanes_min(x):
    for by in (4, 2, 1):
        x = jnp.minimum(x, pltpu.roll(x, by, 0))
    return x


def kernel(
    rows,
    cols,
    cost_hbm,
    image_hbm,
    small_hbm,
    large_hbm,
    out_ref,
    small_ref,
    large_ref,
    own_image,
    mate_image,
    own_raw,
    mate_raw,
    far_raw,
    far_across,
    order,
    totals,
    across_costs,
    down_costs,
    paths,
    lowests,
    large_lines,
    image_lines,
    outbox,
    inbox,
    edge_out,
    edge_in,
    send_sems,
    recv_sems,
    local_sems,
):
    disparities = cost_hbm.shape[1]
    nv = disparities // SUBLANES
    halves = disparities // LANES
    nx, ny = lax.axis_size("gx"), lax.axis_size("gy")
    ix, iy = lax.axis_index("gx"), lax.axis_index("gy")
    nz = nx // CORES
    iz, core = ix // CORES, ix % CORES
    mate = {"gx": iz * CORES + 1 - core}
    own_base = core * cols
    spans = (CORES * cols, rows)
    costs = (across_costs, down_costs)
    lengths = (cols, cols, rows, rows)
    lines = (rows, rows, cols, cols)
    backward = (False, True, False, True)

    place = (iz, nz - 1 - iz, iy, ny - 1 - iy)
    places = (nz, nz, ny, ny)
    hands_on = (core == 1, core == 0, True, True)
    is_last = [place[k] == places[k] - 1 for k in range(4)]

    def next_across(k, by, to_core):
        step = -by if backward[k] else by
        return {"gx": (iz + step) * CORES + to_core}

    def next_down(k, by):
        return {"gy": iy - by if backward[k] else iy + by}

    def prev_across(k, by):
        return next_across(k, -by, 0 if backward[k] else 1)

    def both(*flags):
        result = True
        for flag in flags:
            result = flag if result is True else jnp.logical_and(result, flag)
        return result

    sends = iter(range(SENDS))

    def remote(source, target, recv, device):
        return pltpu.make_async_remote_copy(
            src_ref=source,
            dst_ref=target,
            send_sem=send_sems.at[next(sends)],
            recv_sem=recv_sems.at[recv],
            device_id=device,
            device_id_type=MESH,
        )

    mate_copies = [
        (None, remote(own_image, mate_image, 0, mate)),
        (None, remote(own_raw, mate_raw, 1, mate)),
    ]
    edge_copies, path_copies, far_raw_copies, far_large_copies = [], [], [], []
    forward_copies = {}
    for k in range(4):
        sent = hands_on[k]
        after = places[k] - 1 - place[k]
        near_end = 2 if SKIPS[k] else 1
        if k < 2:
            to = lambda by, k=k: [next_across(k, by, c) for c in range(CORES)]
            same_core = next_across(k, 1, core)
        else:
            to = lambda by, k=k: [next_down(k, by)]
            same_core = next_down(k, 1)
        edge_copies.append(
            [
                (both(sent, after >= 1), remote(edge_out.at[k], edge_in.at[k], 2 + k, device))
                for device in to(1)
            ]
        )
        path_copies.append(
            [
                (both(sent, after >= near_end), remote(outbox.at[k], inbox.at[k], 6 + k, device))
                for device in to(1)
            ]
        )
        if SKIPS[k]:
            path_copies[k] += [
                (both(sent, after == 2), remote(outbox.at[k], inbox.at[k], 6 + k, device))
                for device in to(2)
            ]
            span = spans[k // 2]
            target = far_across.at[core] if k < 2 else far_raw
            far_raw_copies.append([(after == 1, remote(own_raw, target, 10 + k, same_core))])
            far_large_copies.append(
                [
                    (
                        after == 1,
                        remote(
                            large_lines.at[k, pl.ds(span, span)],
                            large_lines.at[k, pl.ds(0, span)],
                            14 + k,
                            same_core,
                        ),
                    )
                ]
            )
            if k < 2:
                here = far_across.at[core]
                forward_copies[k] = [(None, remote(here, here, 18 + k, mate))]
        else:
            far_raw_copies.append([])
            far_large_copies.append([])

    def start(copies):
        for flag, copy in copies:
            if flag is None:
                copy.start()
            else:
                pl.when(flag)(copy.start)

    def drain(copies):
        for flag, copy in copies:
            if flag is None:
                copy.wait_send()
            else:
                pl.when(flag)(copy.wait_send)

    locals_ = [
        pltpu.make_async_copy(source, target, local_sems.at[at])
        for at, (source, target) in enumerate(
            (
                (image_hbm, own_image),
                (small_hbm, small_ref),
                (large_hbm, large_ref),
                *(
                    (cost_hbm.at[:, pl.ds(h * LANES, LANES)], own_raw.at[h])
                    for h in range(halves)
                ),
            )
        )
    ]
    for copy in locals_:
        copy.start()

    barrier = pltpu.get_barrier_semaphore()

    def greet(device):
        pl.semaphore_signal(barrier, inc=1, device_id=device, device_id_type=MESH)

    greet(mate)
    awaited = jnp.int32(1)
    for k in range(4):
        after = places[k] - 1 - place[k]
        ends = both(after == 0, place[k] > 0)
        skips = both(after == 0, place[k] > 1)
        if k < 2:
            pl.when(place[k] > 0)(functools.partial(greet, prev_across(k, 1)))
            awaited += jnp.where(both(hands_on[k], after >= 1), CORES, 0)
            if SKIPS[k]:
                far_only = jnp.logical_not(hands_on[k])
                pl.when(both(ends, far_only))(
                    functools.partial(greet, next_across(k, -1, core))
                )
                awaited += jnp.where(both(far_only, after == 1), 1, 0)
                pl.when(skips)(functools.partial(greet, prev_across(k, 2)))
                awaited += jnp.where(both(hands_on[k], after == 2), CORES, 0)
        else:
            pl.when(place[k] > 0)(functools.partial(greet, next_down(k, -1)))
            awaited += jnp.where(after >= 1, 1, 0)
            if SKIPS[k]:
                pl.when(skips)(functools.partial(greet, next_down(k, -2)))
                awaited += jnp.where(after == 2, 1, 0)

    shape = (disparities, disparities)
    source = lax.broadcasted_iota(jnp.int32, shape, 1)
    target = lax.broadcasted_iota(jnp.int32, shape, 0)
    wanted = target // SUBLANES + nv * (target % SUBLANES)
    order[...] = jnp.where(source == wanted, 1.0, 0.0).astype(jnp.bfloat16)

    for copy in locals_[:3]:
        copy.wait()
    image = own_image[...]
    image_lines[...] = jnp.zeros_like(image_lines)
    image_lines[1, 0:rows, :cols] = image
    image_lines[0, pl.ds(pl.multiple_of(own_base, SUBLANES), cols), :rows] = image.T
    edge_out[...] = jnp.zeros_like(edge_out)
    edge_out[0, 0:1, :rows] = image.T[cols - 1 : cols, :]
    edge_out[1, 0:1, :rows] = image.T[0:1, :]
    edge_out[2, 0:1, :cols] = image[rows - 1 : rows, :]
    edge_out[3, 0:1, :cols] = image[0:1, :]
    for copy in locals_[3:]:
        copy.wait()

    def turn(origin, into, base, axis):
        width = lines[2 * axis]
        group = LANES // width

        def some(index, carry):
            first = index * group
            block = []
            for h in range(halves):
                if axis == 0:
                    parts = [
                        origin[h, pl.ds(first + j, width, stride=cols), :] for j in range(group)
                    ]
                    block.append(jnp.concatenate(parts, axis=0))
                else:
                    at = pl.ds(index * LANES, LANES)
                    block.append(origin[h, at, :])
            block = jnp.concatenate(block, axis=1).astype(jnp.float32).astype(jnp.bfloat16)
            block = lax.dot_general(
                order[...], block, (((1,), (1,)), ((), ())), preferred_element_type=jnp.float32
            )
            for j in range(group):
                moved = pltpu.roll(block, LANES - j * width, 1) if j else block
                into[base + first + j] = moved.reshape(nv, SUBLANES, LANES)
            return carry

        for index in range(rows * cols // LANES):
            some(index, None)

    def turn_across(origin, base):
        turn(origin, across_costs, base, 0)

    def turn_down(origin, base):
        turn(origin, down_costs, base, 1)

    def take_mate():
        for _, copy in mate_copies:
            copy.wait_recv()
        at = pl.ds(pl.multiple_of(cols - own_base, SUBLANES), cols)
        image_lines[0, at, :rows] = mate_image[...].T
        turn_across(mate_raw, spans[0] + cols - own_base)

    pl.semaphore_wait(barrier, awaited)
    start(mate_copies)
    for k in range(4):
        start(edge_copies[k])
    for k in range(4):
        start(far_raw_copies[k])

    pl.when(iz < nz - 1)(lambda: turn_down(own_raw, rows))
    turn_across(own_raw, spans[0] + own_base)
    pl.when(iz == nz - 1)(take_mate)

    sub = lax.broadcasted_iota(jnp.int32, (SUBLANES, LANES), 0)
    lane = lax.broadcasted_iota(jnp.int32, (SUBLANES, LANES), 1)

    def task(k):
        axis = k // 2
        length, width = lengths[k], lines[k]
        group = LANES // width
        small = small_ref[k].astype(jnp.float32)
        large = large_ref[k].astype(jnp.float32)
        step_costs = costs[axis]
        first = place[k] == 0

        @pl.when(jnp.logical_not(first))
        def _():
            edge_copies[k][0][1].wait_recv()

        @pl.when(first)
        def _():
            edge_in[k] = jnp.zeros((SUBLANES, LANES), jnp.float32)

        edge = edge_in[k, 0:1, :]
        if axis == 0:
            own = image_lines[0, : CORES * length, :]
        else:
            own = image_lines[1, :length, :]
        if backward[k]:
            before = jnp.concatenate([own[1:], edge], axis=0)
        else:
            before = jnp.concatenate([edge, own[:-1]], axis=0)
        found = small + (large - small) / (1.0 + GRADIENT_GAIN * jnp.abs(own - before))
        span = spans[axis]
        large_lines[k, span : 2 * span] = found
        start(far_large_copies[k])
        ends = both(is_last[k], jnp.logical_not(first)) if SKIPS[k] else False
        receives = jnp.logical_not(first)
        if SKIPS[k]:
            if axis == 1:

                @pl.when(ends)
                def _():
                    far_raw_copies[k][0][1].wait_recv()
                    turn_down(far_raw, 0)

            pl.when(ends)(far_large_copies[k][0][1].wait_recv)
            receives = jnp.where(is_last[k], place[k] > 1, receives)

        @pl.when(receives)
        def _():
            path_copies[k][0][1].wait_recv()

        @pl.when(jnp.logical_not(receives))
        def _():
            inbox[k] = jnp.zeros(inbox.shape[1:], jnp.float32)

        for v in range(nv):
            packed = inbox[k, v // group]
            shift = (v % group) * width
            paths[k, 0, v] = pltpu.roll(packed, LANES - shift, 1) if shift else packed

        def load(at):
            return [paths[k, at, v] for v in range(nv)]

        def store(at, state):
            for v in range(nv):
                paths[k, at, v] = state[v]

        def step(line, state):
            capped = large_lines[k, pl.ds(line, SUBLANES, stride=0), :]
            under = jnp.where(sub == 0, FAR, pltpu.roll(state[-1], 1, 0))
            over = jnp.where(sub == SUBLANES - 1, FAR, pltpu.roll(state[0], SUBLANES - 1, 0))
            beside = []
            for v in range(nv):
                low = state[v - 1] if v else under
                high = state[v + 1] if v < nv - 1 else over
                beside.append(jnp.minimum(low, high))
            if nv % 4 == 0:
                lowest = tree_min([beside[v] for v in range(nv) if v % 4 in (1, 2)])
            else:
                lowest = tree_min(state)
            lowest = all_sublanes_min(lowest)
            capped = capped + lowest
            fresh = []
            for v in range(nv):
                near = jnp.minimum(state[v], beside[v] + small)
                fresh.append(step_costs[line, v] + jnp.minimum(near, capped))
            return fresh, lowest

        def early(index, carry):
            state = load(0)
            for part in range(UNROLL):
                at = index * UNROLL + part
                if backward[k]:
                    at = jnp.where(at < span, span - 1 - at, 3 * span - 1 - at)
                state, _ = step(at, state)
            store(0, state)
            return carry

        def late(index, carry):
            state = load(index * UNROLL)
            for part in range(UNROLL):
                at = index * UNROLL + part
                line = length - 1 - at if backward[k] else at
                state, lowest = step(span + (own_base if axis == 0 else 0) + line, state)
                store(at + 1, state)
                lowests[k, at] = lowest
            return carry

        begin = jnp.where(ends, 0, span // UNROLL) if SKIPS[k] else span // UNROLL
        end = span // UNROLL
        if axis == 0:
            end = jnp.where(hands_on[k], (span + length) // UNROLL, end)
        lax.fori_loop(begin, end, early, 0)
        lax.fori_loop(0, length // UNROLL, late, 0)

        after = places[k] - 1 - place[k]

        @pl.when(both(hands_on[k], after >= (2 if SKIPS[k] else 1)))
        def _():
            above = lowests[k, length - 1]
            sent = [part - above for part in load(length)]
            for slot in range(nv // group):
                packed = sent[slot * group]
                for g in range(1, group):
                    moved = pltpu.roll(sent[slot * group + g], g * width, 1)
                    packed = jnp.where(lane >= g * width, moved, packed)
                outbox[k, slot] = packed

        start(path_copies[k])

    def total(axis):
        k = 2 * axis
        width = lines[k]
        group = LANES // width

        def some(index, carry):
            packed = [None] * nv
            for j in range(group):
                line = index * group + j
                back = lengths[k] - 1 - line
                above = lowests[k, line] + lowests[k + 1, back]
                for v in range(nv):
                    part = paths[k, line + 1, v] + paths[k + 1, back + 1, v] - above
                    if j:
                        part = jnp.where(lane >= j * width, pltpu.roll(part, j * width, 1), packed[v])
                    packed[v] = part
            for h in range(halves):
                per = LANES // SUBLANES
                turned = jnp.concatenate(packed[h * per : (h + 1) * per], axis=0).T
                if axis == 0:
                    for j in range(group):
                        at = pl.ds(index * group + j, width, stride=cols)
                        totals[axis, h, at, :] = turned[j * width : (j + 1) * width]
                else:
                    at = pl.ds(index * LANES, LANES)
                    totals[axis, h, at, :] = turned
            return carry

        for index in range(rows * cols // LANES):
            some(index, None)

    turns = max(nz, ny)
    down_done = jnp.maximum(place[2], place[3])
    turn_left = jnp.where(places[1] - 1 - place[1] >= 2, place[1], turns)
    ends_left = both(is_last[1], place[1] > 0)

    def one_turn(turn_at, carry):
        @pl.when(both(turn_at == turns - 1, ends_left))
        def _():
            forward_copies[1][0][1].wait_recv()
            for c in range(CORES):
                turn_across(far_across.at[c], c * cols)

        pl.when(turn_at == turn_left)(lambda: task(1))
        pl.when(both(turn_at == 0, iz == nz - 1))(lambda: turn_down(own_raw, rows))
        pl.when(turn_at == place[2])(lambda: task(2))
        pl.when(turn_at == place[3])(lambda: task(3))
        pl.when(both(turn_at == 0, iz < nz - 1))(take_mate)

        @pl.when(both(turn_at == turns - 2, ends_left))
        def _():
            far_raw_copies[1][0][1].wait_recv()
            start(forward_copies[1])

        pl.when(turn_at == down_done)(lambda: total(1))
        pl.when(turn_at == place[0])(lambda: task(0))
        return carry

    lax.fori_loop(0, turns + 1, one_turn, 0)
    total(0)
    rest = jnp.concatenate([totals[0, h] + totals[1, h] for h in range(halves)], axis=1)
    rest = rest * OUT_SCALE
    result = None
    for part in range(3):
        piece = rest.astype(jnp.bfloat16)
        moved = lax.dot_general(
            piece, order[...], (((1,), (0,)), ((), ())), preferred_element_type=jnp.float32
        )
        result = moved if part == 0 else result + moved
        if part < 2:
            rest = rest - piece.astype(jnp.float32)
    out_ref[...] = result

    drain(mate_copies)
    pl.when(ends_left)(forward_copies[1][0][1].wait_send)
    for k in range(4):
        drain(edge_copies[k])
        drain(path_copies[k])
        drain(far_raw_copies[k])
        drain(far_large_copies[k])


def on_device(cost_volume, left_image, p_small, p_large):
    rows, cols, disparities = cost_volume.shape
    nv = disparities // SUBLANES
    longest = max(rows, cols)
    packed = nv * longest // LANES
    halves = disparities // LANES
    block = (halves, rows * cols, LANES)
    hbm = pl.BlockSpec(memory_space=pltpu.HBM)
    vmem = pl.BlockSpec(memory_space=pltpu.VMEM)
    total = pl.pallas_call(
        functools.partial(kernel, rows, cols),
        out_shape=jax.ShapeDtypeStruct((rows * cols, disparities), jnp.float32),
        in_specs=[hbm] * 4,
        out_specs=vmem,
        scratch_shapes=[
            pltpu.SMEM((4,), jnp.int32),
            pltpu.SMEM((4,), jnp.int32),
            pltpu.VMEM((rows, cols), jnp.float32),
            pltpu.VMEM((rows, cols), jnp.float32),
            pltpu.VMEM(block, jnp.int32),
            pltpu.VMEM(block, jnp.int32),
            pltpu.VMEM(block, jnp.int32),
            pltpu.VMEM((CORES, *block), jnp.int32),
            pltpu.VMEM((disparities, disparities), jnp.bfloat16),
            pltpu.VMEM((2, halves, rows * cols, LANES), jnp.float32),
            pltpu.VMEM((2 * CORES * cols, nv, SUBLANES, LANES), jnp.float32),
            pltpu.VMEM((2 * rows, nv, SUBLANES, LANES), jnp.float32),
            pltpu.VMEM((4, longest + 1, nv, SUBLANES, LANES), jnp.float32),
            pltpu.VMEM((4, longest, SUBLANES, LANES), jnp.float32),
            pltpu.VMEM((4, 2 * CORES * longest, LANES), jnp.float32),
            pltpu.VMEM((2, CORES * longest, LANES), jnp.float32),
            pltpu.VMEM((4, packed, SUBLANES, LANES), jnp.float32),
            pltpu.VMEM((4, packed, SUBLANES, LANES), jnp.float32),
            pltpu.VMEM((4, SUBLANES, LANES), jnp.float32),
            pltpu.VMEM((4, SUBLANES, LANES), jnp.float32),
            pltpu.SemaphoreType.DMA((SENDS,)),
            pltpu.SemaphoreType.DMA((20,)),
            pltpu.SemaphoreType.DMA((3 + halves,)),
        ],
        compiler_params=pltpu.CompilerParams(
            collective_id=0, has_side_effects=True, vmem_limit_bytes=VMEM_BYTES
        ),
    )(
        *(
            pltpu.with_memory_space_constraint(array, pltpu.HBM)
            for array in (
                cost_volume.reshape(rows * cols, disparities),
                left_image,
                p_small,
                p_large,
            )
        )
    )
    return total.reshape(rows, cols, disparities)


def solution(mesh):
    in_specs = (P("gy", "gx", None), P("gy", "gx"), P(), P())
    out_specs = P("gy", "gx", None)
    return jax.shard_map(
        on_device, mesh=mesh, in_specs=in_specs, out_specs=out_specs, check_vma=False
    )
```

time: 22.5 us -> 21.8 us (0.969)
  Pallas kernels: 21.5 us -> 20.9 us
    pallas_call x1, Pallas kernels: 21.5 us -> 20.9 us  [on_device(): pl.pallas_call(functools.partial(kernel, rows, cols), out_shape=jax.Shape...]
where the time goes in v3:
time: 21.8 us; the launch traced here: 21.6 us
  Pallas kernels  20.9 us (96%)
  local copies, waits for them, and re-layouts  0.71 us (3%)
    pallas_call x1, Pallas kernels, on_device(): pl.pallas_call(functools.partial(kernel, rows, cols), out_shape=jax.Shape...  20.9 us
    unnamed x1, local copies, waits for them, and re-layouts  0.71 us

profile of v3, /device:TPU:0, one launch (start us, length us, event | category | flops | bytes accessed | tf_op | source)
XLA Modules:
  0.0 21.6 jit_solution(18336637067186256348)
XLA Ops:
  0.0 20.9 %shard_map.46 = f32[256,256]{1,0:T(8,128)S(1)} custom-call(s32[256,256]{1,0:T(8,128)} %bitcast.3, f32[16,16]{1,0:T(8,128)} %image_hbm.1, s32[4]{0:T(128)} %small_hbm.1, s32[4]{0:T(128)} %large_hbm.1), custom_call_target="tpu_custom_call" | custom-call | tf_op jit(solution)/shard_map/pallas_call | solution.py:525
  20.9 0.7 %copy.6 = f32[16,16,256]{2,1,0:T(8,128)} copy(f32[16,16,256]{2,1,0:T(8,128)S(1)} %bitcast.2) | data formatting | bytes 524288

commit v4 on v3

--- a/solution.py
+++ b/solution.py
@@ -305,36 +305,40 @@
     sub = lax.broadcasted_iota(jnp.int32, (SUBLANES, LANES), 0)
     lane = lax.broadcasted_iota(jnp.int32, (SUBLANES, LANES), 1)
 
+    def penalties(k):
+        axis = k // 2
+        small = small_ref[k].astype(jnp.float32)
+        large = large_ref[k].astype(jnp.float32)
+        span = spans[axis]
+        own = image_lines[axis, :span, :]
+        edge = edge_in[k, 0:1, :]
+        if backward[k]:
+            before = jnp.concatenate([own[1:], edge], axis=0)
+        else:
+            before = jnp.concatenate([edge, own[:-1]], axis=0)
+        large_lines[k, span : 2 * span] = small + (large - small) / (
+            1.0 + GRADIENT_GAIN * jnp.abs(own - before)
+        )
+
+    def early_penalties(k):
+        edge_in[k] = jnp.zeros((SUBLANES, LANES), jnp.float32)
+        penalties(k)
+        start(far_large_copies[k])
+
+    def later_penalties(k):
+        edge_copies[k][0][1].wait_recv()
+        penalties(k)
+        start(far_large_copies[k])
+
     def task(k):
         axis = k // 2
         length, width = lengths[k], lines[k]
         group = LANES // width
         small = small_ref[k].astype(jnp.float32)
-        large = large_ref[k].astype(jnp.float32)
         step_costs = costs[axis]
+        span = spans[axis]
         first = place[k] == 0
-
-        @pl.when(jnp.logical_not(first))
-        def _():
-            edge_copies[k][0][1].wait_recv()
-
-        @pl.when(first)
-        def _():
-            edge_in[k] = jnp.zeros((SUBLANES, LANES), jnp.float32)
-
-        edge = edge_in[k, 0:1, :]
-        if axis == 0:
-            own = image_lines[0, : CORES * length, :]
-        else:
-            own = image_lines[1, :length, :]
-        if backward[k]:
-            before = jnp.concatenate([own[1:], edge], axis=0)
-        else:
-            before = jnp.concatenate([edge, own[:-1]], axis=0)
-        found = small + (large - small) / (1.0 + GRADIENT_GAIN * jnp.abs(own - before))
-        span = spans[axis]
-        large_lines[k, span : 2 * span] = found
-        start(far_large_copies[k])
+        pl.when(first)(lambda: early_penalties(k))
         ends = both(is_last[k], jnp.logical_not(first)) if SKIPS[k] else False
         receives = jnp.logical_not(first)
         if SKIPS[k]:
@@ -468,7 +472,7 @@
     ends_left = both(is_last[1], place[1] > 0)
 
     def one_turn(turn_at, carry):
-        @pl.when(both(turn_at == turns - 1, ends_left))
+        @pl.when(both(turn_at == turns, ends_left))
         def _():
             forward_copies[1][0][1].wait_recv()
             for c in range(CORES):
@@ -487,6 +491,12 @@
 
         pl.when(turn_at == down_done)(lambda: total(1))
         pl.when(turn_at == place[0])(lambda: task(0))
+
+        @pl.when(turn_at == 0)
+        def _():
+            for k in range(4):
+                pl.when(place[k] > 0)(functools.partial(later_penalties, k))
+
         return carry
 
     lax.fori_loop(0, turns + 1, one_turn, 0)

time: 21.8 us -> 19.7 us (0.904)
  Pallas kernels: 20.9 us -> 18.8 us
    pallas_call x1, Pallas kernels: 20.9 us -> 18.8 us  [on_device(): pl.pallas_call(functools.partial(kernel, rows, cols), out_shape=jax.Shape...]
where the time goes in v4:
time: 19.7 us; the launch traced here: 19.5 us
  Pallas kernels  18.8 us (95%)
  local copies, waits for them, and re-layouts  0.71 us (4%)
    pallas_call x1, Pallas kernels, on_device(): pl.pallas_call(functools.partial(kernel, rows, cols), out_shape=jax.Shape...  18.8 us
    unnamed x1, local copies, waits for them, and re-layouts  0.71 us

profile of v4, /device:TPU:0, one launch (start us, length us, event | category | flops | bytes accessed | tf_op | source)
XLA Modules:
  0.0 19.5 jit_solution(8882758847990634432)
XLA Ops:
  0.0 18.8 %shard_map.46 = f32[256,256]{1,0:T(8,128)S(1)} custom-call(s32[256,256]{1,0:T(8,128)} %bitcast.3, f32[16,16]{1,0:T(8,128)} %image_hbm.1, s32[4]{0:T(128)} %small_hbm.1, s32[4]{0:T(128)} %large_hbm.1), custom_call_target="tpu_custom_call" | custom-call | tf_op jit(solution)/shard_map/pallas_call | solution.py:535
  18.8 0.7 %copy.6 = f32[16,16,256]{2,1,0:T(8,128)} copy(f32[16,16,256]{2,1,0:T(8,128)S(1)} %bitcast.2) | data formatting | bytes 524288
